TPU v7x, 32 devices: a whole 2x2x4 slice. The times are simulated.
32 devices in a mesh: img: 4 (over z), seq: 4 (over x, core), head: 2 (over y).
Axes of the slice: x: 2, y: 2, z: 4, core: 2. Of those that a mesh axis runs over, the one named last changes fastest.
Arguments:
- self_qkv: bfloat16 [4, 1024, 3072], P('img', ('seq', 'head')), may hold values from -12 to 12
- cross_query: bfloat16 [4, 1024, 1024], P('img', ('seq', 'head')), may hold values from -12 to 12
- thermal_kv: bfloat16 [4, 8, 256, 2048], P('img', ('seq', 'head')), may hold values from -12 to 12
- owners: int32 [4], P('img'), may hold values from 0 to 7
- grad_out: bfloat16 [4, 1024, 1024], P('img', ('seq', 'head')), may hold values from -6 to 6
Outputs:
- combined: bfloat16 [4, 1024, 1024], P('img', ('seq', 'head'))
- grad_qkv: bfloat16 [4, 1024, 3072], P('img', ('seq', 'head'))
- grad_cross_query: bfloat16 [4, 1024, 1024], P('img', ('seq', 'head'))
- grad_thermal: bfloat16 [4, 256, 2048], P('img', ('seq', 'head'))
All inputs are finite; a program needn't handle non-finite values.
Results may differ from a plain program's by a relative error of at most 0.012.
The roundings to bfloat16 on the way count: a program that leaves them out, or rounds other values in their place, can miss the bound.
Values may be sent and summed in bfloat16 or wider, within the bound.
No kernel may reach another device: no remote copies, remote signals or barrier semaphores. Data moves between devices by JAX's collectives and lax.ppermute only.
A program may use at most 128 MiB of HBM per device.

v0:
```python
import math
import jax
import jax.numpy as jnp
from jax import lax
from jax.sharding import PartitionSpec as P

HEADS = 16
HD = 64


def spread(block, axis, owner):
    block = jnp.where(lax.axis_index(axis) == owner, block, jnp.zeros_like(block))
    return lax.psum(block, axis)


def log_total(scores):
    row_max = jnp.max(scores, axis=-1, keepdims=True)
    return row_max + jnp.log(jnp.sum(jnp.exp(scores - row_max), axis=-1, keepdims=True))


def output_delta(upstream, mixed):
    return jnp.sum(upstream.astype(jnp.float32) * mixed, axis=-1).T[:, :, None]


def cross_block(cross_heads, upstream, thermal_keys, thermal_values, score_scale):
    cross_scores = (
        jnp.einsum("qhd,khd->hqk", cross_heads, thermal_keys, preferred_element_type=jnp.float32)
        * score_scale
    )
    cross_lse = log_total(cross_scores)
    cross_probs = jnp.exp(cross_scores - cross_lse).astype(jnp.bfloat16)
    cross_mixed = jnp.einsum(
        "hqk,khd->qhd", cross_probs, thermal_values, preferred_element_type=jnp.float32
    )
    cross_dprobs = jnp.einsum(
        "qhd,khd->hqk", upstream, thermal_values, preferred_element_type=jnp.float32
    )
    cross_delta = output_delta(upstream, cross_mixed)
    cross_dscores = (
        cross_probs.astype(jnp.float32) * (cross_dprobs - cross_delta) * score_scale
    ).astype(jnp.bfloat16)
    cross_dq = jnp.einsum(
        "hqk,khd->qhd", cross_dscores, thermal_keys, preferred_element_type=jnp.float32
    )
    return (cross_mixed, cross_probs, cross_dscores, cross_dq)


def thermal_sums(cross_probs, cross_dscores, cross_heads, upstream, row_span):
    key_grad = jnp.einsum(
        "hqk,qhd->khd", cross_dscores, cross_heads, preferred_element_type=jnp.float32
    )
    value_grad = jnp.einsum(
        "hqk,qhd->khd", cross_probs, upstream, preferred_element_type=jnp.float32
    )
    width = key_grad.shape[1] * key_grad.shape[2]
    return jnp.concatenate(
        [key_grad.reshape(row_span, width), value_grad.reshape(row_span, width)], axis=1
    )


def body(self_qkv, cross_query, thermal_kv, owners, grad_out):
    tokens_here = self_qkv.shape[1]
    model_width = cross_query.shape[2]
    head_devices = lax.axis_size("head")
    heads_local = HEADS // head_devices
    local_width = heads_local * HD
    score_scale = 1.0 / math.sqrt(HD)
    thermal_rows = thermal_kv.shape[2]
    packed = self_qkv[0].reshape(tokens_here, 3, head_devices, local_width)
    by_heads = lax.all_to_all(packed, "head", split_axis=2, concat_axis=0, tiled=True)
    row_count = by_heads.shape[0]
    query_flat = by_heads[:, 0, 0]
    keys_all, values_all = (
        lax.all_gather(by_heads[:, 1, 0], "seq", axis=0, tiled=True),
        lax.all_gather(by_heads[:, 2, 0], "seq", axis=0, tiled=True),
    )
    key_rows = keys_all.shape[0]
    query_here = query_flat.reshape(row_count, heads_local, HD)
    keys_heads = keys_all.reshape(key_rows, heads_local, HD)
    values_heads = values_all.reshape(key_rows, heads_local, HD)
    scores = (
        jnp.einsum("qhd,khd->hqk", query_here, keys_heads, preferred_element_type=jnp.float32)
        * score_scale
    )
    self_lse = log_total(scores)
    self_probs = jnp.exp(scores - self_lse).astype(jnp.bfloat16)
    attended_wide = jnp.einsum(
        "hqk,khd->qhd", self_probs, values_heads, preferred_element_type=jnp.float32
    )
    attended_heads = attended_wide.astype(jnp.bfloat16)
    attended = lax.all_to_all(
        attended_heads.reshape(row_count, 1, local_width),
        "head",
        split_axis=0,
        concat_axis=1,
        tiled=True,
    )
    attended = attended.reshape(tokens_here, model_width)
    thermal = spread(thermal_kv[0, 0], ("seq", "head"), owners[0])
    cross_in = (attended.astype(jnp.float32) + cross_query[0].astype(jnp.float32)).astype(
        jnp.bfloat16
    )
    cross_heads = cross_in.reshape(tokens_here, HEADS, HD)
    upstream = grad_out[0].reshape(tokens_here, HEADS, HD)
    thermal_keys = thermal[:, :model_width].reshape(thermal_rows, HEADS, HD)
    thermal_values = thermal[:, model_width:].reshape(thermal_rows, HEADS, HD)
    cross_mixed, cross_probs, cross_dscores, cross_dq = cross_block(
        cross_heads, upstream, thermal_keys, thermal_values, score_scale
    )
    combined = (
        attended.astype(jnp.float32) + cross_mixed.reshape(tokens_here, model_width)
    ).astype(jnp.bfloat16)
    cross_dq = cross_dq.reshape(tokens_here, model_width)
    group_devices = lax.axis_size("seq") * head_devices
    grad_thermal = lax.psum_scatter(
        thermal_sums(
            cross_probs,
            cross_dscores,
            cross_heads,
            upstream,
            lax.axis_size(("seq", "head")) * (thermal_rows // group_devices),
        ),
        ("seq", "head"),
        scatter_dimension=0,
        tiled=True,
    ).astype(jnp.bfloat16)
    grad_cross = cross_dq.astype(jnp.bfloat16)
    attended_grad = (grad_out[0].astype(jnp.float32) + cross_dq).astype(jnp.bfloat16)
    grad_heads = lax.all_to_all(
        attended_grad.reshape(tokens_here, head_devices, local_width),
        "head",
        split_axis=1,
        concat_axis=0,
        tiled=True,
    )
    grad_flat = grad_heads.reshape(row_count, local_width)
    grad_here = grad_flat.reshape(row_count, heads_local, HD)
    self_dprobs = jnp.einsum(
        "qhd,khd->hqk", grad_here, values_heads, preferred_element_type=jnp.float32
    )
    self_delta = output_delta(grad_here, attended_wide)
    self_dscores = (
        self_probs.astype(jnp.float32) * (self_dprobs - self_delta) * score_scale
    ).astype(jnp.bfloat16)
    query_grad = jnp.einsum(
        "hqk,khd->qhd", self_dscores, keys_heads, preferred_element_type=jnp.float32
    )
    query_grad = query_grad.reshape(row_count, local_width)
    key_grad = jnp.einsum(
        "hqk,qhd->khd", self_dscores, query_here, preferred_element_type=jnp.float32
    )
    value_grad = jnp.einsum(
        "hqk,qhd->khd", self_probs, grad_here, preferred_element_type=jnp.float32
    )
    own_grads = lax.psum_scatter(
        jnp.concatenate(
            [
                key_grad.reshape(lax.axis_size("seq") * row_count, local_width),
                value_grad.reshape(lax.axis_size("seq") * row_count, local_width),
            ],
            axis=1,
        ),
        "seq",
        scatter_dimension=0,
        tiled=True,
    )
    key_own = own_grads[:, :local_width]
    value_own = own_grads[:, local_width:]
    stacked = jnp.stack([query_grad, key_own, value_own], axis=1).astype(jnp.bfloat16)
    stacked = stacked.reshape(row_count, 3, 1, local_width)
    grad_qkv = lax.all_to_all(stacked, "head", split_axis=0, concat_axis=2, tiled=True).reshape(
        tokens_here, 3 * model_width
    )
    return (combined[None], grad_qkv[None], grad_cross[None], grad_thermal[None])


def solution(mesh):
    placed = (
        P("img", ("seq", "head"), None),
        P("img", ("seq", "head"), None),
        P("img", ("seq", "head"), None, None),
        P("img"),
        P("img", ("seq", "head"), None),
    )
    return jax.shard_map(
        body,
        mesh=mesh,
        in_specs=placed,
        out_specs=(
            P("img", ("seq", "head"), None),
            P("img", ("seq", "head"), None),
            P("img", ("seq", "head"), None),
            P("img", ("seq", "head"), None),
        ),
        check_vma=False,
    )
```

profile of v0, /device:TPU:0, one launch (start us, length us, event | category | flops | bytes accessed | tf_op | source)
XLA Modules:
  0.0 235.7 jit_solution(8329508114149124383)
XLA Ops:
  8.1 1.6 copy.134
  9.9 14.9 %all_to_all.57 = bf16[128,3,2,512]{3,0,1,2:T(8,128)(2,1)S(1)} all-to-all(bf16[128,3,2,512]{3,0,1,2:T(8,128)(2,1)S(1)} %copy.135), channel_id=1, replica_groups=mesh['img'=4,'seq'=4,'head'=2] {'head'}, dimensions={2} | all-to-all | bytes 1572864 | tf_op jit(solution)/shard_map/all_to_all | solution.py:70
  29.9 13.5 %all-gather.5.cloned.1.call-done = bf16[1024,1,1,512]{3,0,1,2:T(8,128)(2,1)} async-done(((bf16[256,1,1,512]{3,0,1,2:T(8,128)(2,1)}), bf16[1024,1,1,512]{3,0,1,2:T(8,128)(2,1)}) %all-gather.5.cloned.1.call-update) | async-done | bytes 1048592 | tf_op jit(solution)/shard_map/all_gather | solution.py:74
  43.4 1.5 copy.138
  44.9 1.4 multiply_reduce_fusion
  46.3 1.7 exponential_reduce_fusion
  48.0 2.7 %exponential_convert_fusion = bf16[8,256,1024]{2,1,0:T(8,128)(2,1)} fusion(f32[8,256,1024]{2,1,0:T(8,128)S(1)} %get-tuple-element.40, f32[8,256]{1,0:T(8,128)S(1)} %log_add_fusion.1), kind=kLoop, calls=%fused_computation.1 | loop fusion | flops 6291456 | bytes 12591104 | tf_op jit(solution)/shard_map/convert_element_type | solution.py:86
  50.7 11.8 %all-gather.7.cloned.1.call-done = bf16[1024,1,1,512]{3,0,1,2:T(8,128)(2,1)} async-done(((bf16[256,1,1,512]{3,0,1,2:T(8,128)(2,1)}), bf16[1024,1,1,512]{3,0,1,2:T(8,128)(2,1)}) %all-gather.7.cloned.1.call-update) | async-done | bytes 1048592 | tf_op jit(solution)/shard_map/all_gather | solution.py:75
  62.5 1.5 copy.139
  64.0 4.8 %fusion.10 = (bf16[256,8,64]{0,2,1:T(8,128)(2,1)S(1)}, f32[256,8,64]{0,2,1:T(8,128)}) fusion(bf16[8,256,1024]{2,1,0:T(8,128)(2,1)} %exponential_convert_fusion, bf16[1024,8,64]{0,2,1:T(8,128)(2,1)S(1)} %bitcast.102), kind=kOutput, calls=%fused_computation.33 | convolution fusion | flops 268566528 | bytes 6029312 | tf_op jit(solution)/shard_map/hqk,khd->qhd/dot_general | solution.py:87
  71.1 3.4 %all-to-all-start.1 = ((bf16[2,2,32768]{2,1,0:T(2,128)(2,1)}), bf16[2,2,32768]{2,1,0:T(2,128)(2,1)S(1)}, u32[]{:S(2)}, u32[]{:S(2)}) async-start(bf16[2,2,32768]{2,1,0:T(2,128)(2,1)} %reshape.190), calls=%async_computation.1 | async-start | bytes 524288 | tf_op jit(solution)/shard_map/all_to_all | solution.py:91
  74.6 18.7 %all-reduce.2.cloned.1.call-done = bf16[256,2048]{1,0:T(8,128)(2,1)} async-done(((bf16[256,2048]{1,0:T(8,128)(2,1)}), bf16[256,2048]{1,0:T(8,128)(2,1)}) %all-reduce.2.cloned.1.call-update) | async-done | bytes 1048592 | tf_op jit(solution)/shard_map/psum | solution.py:13
  93.3 2.1 fusion.8
  95.6 1.4 copy.143
  102.5 1.6 fusion.1
  105.4 7.6 %all_to_all.58 = bf16[128,2,512]{0,2,1:T(8,128)(2,1)S(1)} all-to-all(bf16[128,2,512]{0,2,1:T(8,128)(2,1)S(1)} %add_convert_fusion), channel_id=1, replica_groups=mesh['img'=4,'seq'=4,'head'=2] {'head'}, dimensions={1} | all-to-all | bytes 524288 | tf_op jit(solution)/shard_map/all_to_all | solution.py:129
  115.1 4.5 %fusion.11 = f32[8,64,1024]{2,1,0:T(8,128)} fusion(bf16[256,8,64]{0,2,1:T(8,128)(2,1)S(1)} %reshape_reshape.3, bf16[8,256,1024]{2,1,0:T(8,128)(2,1)} %exponential_convert_fusion), kind=kOutput, calls=%fused_computation.34 | convolution fusion | flops 268435456 | bytes 6553600 | tf_op jit(solution)/shard_map/hqk,qhd->khd/dot_general | solution.py:152
  119.7 1.9 multiply_convert_fusion
  121.7 1.9 copy-done.1
  123.6 2.2 fusion.12
  125.8 3.0 %copy.151 = f32[1024,512]{1,0:T(8,128)} copy(f32[1024,512]{0,1:T(8,128)} %bitcast.105) | data formatting | bytes 4194304 | tf_op jit(solution)/shard_map/reshape | solution.py:158
  128.8 2.9 %copy.152 = f32[1024,512]{1,0:T(8,128)} copy(f32[1024,512]{0,1:T(8,128)} %bitcast.104) | data formatting | bytes 4194304 | tf_op jit(solution)/shard_map/reshape | solution.py:159
  131.7 4.7 %pad_maximum_fusion = f32[1024,1024]{1,0:T(8,128)} fusion(f32[1024,512]{1,0:T(8,128)} %copy.152, f32[1024,512]{1,0:T(8,128)} %copy.151), kind=kLoop, calls=%fused_computation.4 | loop fusion | flops 1048576 | bytes 8388608 | tf_op jit(solution)/shard_map/concatenate | solution.py:156
  136.5 2.5 %fusion.4 = f32[16,64,256]{2,1,0:T(8,128)} fusion(bf16[16,128,256]{2,1,0:T(8,128)(2,1)S(1)} %fusion.1, f32[128,16,64]{0,2,1:T(8,128)} %bitcast.107, bf16[128,16,64]{0,2,1:T(8,128)(2,1)} %bitcast.125), kind=kOutput, calls=%fused_computation.29 | convolution fusion | flops 67502080 | bytes 2883584 | tf_op jit(solution)/shard_map/hqk,qhd->khd/dot_general | solution.py:49
  139.0 2.6 %copy.157 = f32[256,1024]{1,0:T(8,128)} copy(f32[256,1024]{0,1:T(8,128)} %bitcast.117) | data formatting | bytes 2097152 | tf_op jit(solution)/shard_map/reshape | solution.py:57
  143.2 3.8 %pad_maximum_fusion.1 = f32[256,2048]{1,0:T(8,128)} fusion(f32[256,1024]{1,0:T(8,128)} %copy.158, f32[256,1024]{1,0:T(8,128)} %copy.157), kind=kLoop, calls=%fused_computation.5 | loop fusion | flops 524288 | bytes 4194304 | tf_op jit(solution)/shard_map/concatenate | solution.py:56
  149.1 3.6 %convolution_convert_fusion = bf16[8,256,64]{1,2,0:T(8,128)(2,1)S(1)} fusion(bf16[8,256,1024]{2,1,0:T(8,128)(2,1)} %copy-done.1, bf16[1024,8,64]{0,2,1:T(8,128)(2,1)S(1)} %bitcast.101), kind=kOutput, calls=%fused_computation.13 | convolution fusion | flops 268566528 | bytes 5505024 | tf_op jit(solution)/shard_map/hqk,khd->qhd/dot_general | solution.py:145
  152.8 27.6 %reduce-scatter.3.cloned.1.call-done = f32[256,1024]{1,0:T(8,128)} async-done(((f32[1024,1024]{1,0:T(8,128)}), f32[256,1024]{1,0:T(8,128)}) %reduce-scatter.3.cloned.1.call-update) | async-done | bytes 1048592 | tf_op jit(solution)/shard_map/reduce_scatter | solution.py:155
  181.9 1.7 copy.154
  183.5 3.6 %all-to-all-start.3 = ((bf16[256,3,1,512]{3,1,2,0:T(4,128)(2,1)}), bf16[256,3,1,512]{3,1,2,0:T(4,128)(2,1)S(1)}, u32[]{:S(2)}, u32[]{:S(2)}) async-start(bf16[256,3,1,512]{3,1,2,0:T(4,128)(2,1)} %copy.154), calls=%async_computation.4 | async-start | bytes 2097152 | tf_op jit(solution)/shard_map/all_to_all | solution.py:171
  187.1 38.1 %reduce-scatter.5.cloned.1.call-done = f32[32,2048]{1,0:T(8,128)} async-done(((f32[256,2048]{1,0:T(8,128)}), f32[32,2048]{1,0:T(8,128)}) %reduce-scatter.5.cloned.1.call-update) | async-done | bytes 262160 | tf_op jit(solution)/shard_map/reduce_scatter | solution.py:115
  225.2 1.6 convert_bitcast_fusion
  (92 shorter events, 23.0 us)
Async XLA Ops:
  8.0 19.3 %copy-start.17 = (bf16[1,1,256,2048]{3,2,1,0:T(8,128)(2,1)S(1)}, bf16[1,1,256,2048]{3,2,1,0:T(8,128)(2,1)}, u32[]{:S(2)}) copy-start(bf16[1,1,256,2048]{3,2,1,0:T(8,128)(2,1)} %param.7) | copy-start | bytes 3145732
  8.0 35.4 %all-gather.5.cloned.1.call-start = ((), (), s32[]{:S(2)}) async-start(), calls=%async_computation.9 | async-start | bytes 1310720 | tf_op jit(solution)/shard_map/all_gather | solution.py:74
  9.9 18.5 %copy-start.18 = (bf16[1,128,1024]{2,1,0:T(8,128)(2,1)S(1)}, bf16[1,128,1024]{2,1,0:T(8,128)(2,1)}, u32[]{:S(2)}) copy-start(bf16[1,128,1024]{2,1,0:T(8,128)(2,1)} %param.9) | copy-start | bytes 786436
  24.9 4.7 %copy-start.20 = (bf16[1,128,1024]{2,1,0:T(8,128)(2,1)S(1)}, bf16[1,128,1024]{2,1,0:T(8,128)(2,1)}, u32[]{:S(2)}) copy-start(bf16[1,128,1024]{2,1,0:T(8,128)(2,1)} %param.6) | copy-start | bytes 786436
  25.8 36.6 %all-gather.7.cloned.1.call-start = ((), (), s32[]{:S(2)}) async-start(), calls=%async_computation.10 | async-start | bytes 1310720 | tf_op jit(solution)/shard_map/all_gather | solution.py:75
  26.6 66.7 %all-reduce.2.cloned.1.call-start = ((), (), s32[]{:S(2)}) async-start(), calls=%async_computation.6 | async-start | bytes 2097152 | tf_op jit(solution)/shard_map/psum | solution.py:13
  28.6 73.9 %copy-start.9 = (bf16[1,128,1024]{1,2,0:T(8,128)(2,1)}, bf16[1,128,1024]{1,2,0:T(8,128)(2,1)S(1)}, u32[]{:S(2)}) copy-start(bf16[1,128,1024]{1,2,0:T(8,128)(2,1)S(1)} %copy.148) | copy-start | bytes 786436
  29.7 69.6 %copy-start.13 = (bf16[1,128,1024]{1,2,0:T(8,128)(2,1)}, bf16[1,128,1024]{1,2,0:T(8,128)(2,1)S(1)}, u32[]{:S(2)}) copy-start(bf16[1,128,1024]{1,2,0:T(8,128)(2,1)S(1)} %copy.144) | copy-start | bytes 786436
  29.9 16.4 %copy-start.11 = (bf16[256,1,1,512]{0,3,2,1:T(8,128)(2,1)}, bf16[256,1,1,512]{0,3,2,1:T(8,128)(2,1)S(1)}, u32[]{:S(2)}) copy-start(bf16[256,1,1,512]{0,3,2,1:T(8,128)(2,1)S(1)} %copy.137) | copy-start | bytes 786436
  64.0 31.4 %copy-start.2 = (bf16[1024,1,1,512]{0,3,2,1:T(8,128)(2,1)}, bf16[1024,1,1,512]{0,3,2,1:T(8,128)(2,1)S(1)}, u32[]{:S(2)}) copy-start(bf16[1024,1,1,512]{0,3,2,1:T(8,128)(2,1)S(1)} %copy.139) | copy-start | bytes 3145732
  71.1 25.9 %all-to-all-start.1 = ((bf16[2,2,32768]{2,1,0:T(2,128)(2,1)}), bf16[2,2,32768]{2,1,0:T(2,128)(2,1)S(1)}, u32[]{:S(2)}, u32[]{:S(2)}) async-start(bf16[2,2,32768]{2,1,0:T(2,128)(2,1)} %reshape.190), calls=%async_computation.1 | async-start | bytes 524288 | tf_op jit(solution)/shard_map/all_to_all | solution.py:91
  74.6 105.9 %reduce-scatter.3.cloned.1.call-start = ((), (), s32[]{:S(2)}) async-start(), calls=%async_computation.7 | async-start | bytes 5242880 | tf_op jit(solution)/shard_map/reduce_scatter | solution.py:155
  95.6 5.1 %copy-start.6 = (bf16[256,1024]{0,1:T(8,128)(2,1)}, bf16[256,1024]{0,1:T(8,128)(2,1)S(1)}, u32[]{:S(2)}) copy-start(bf16[256,1024]{0,1:T(8,128)(2,1)S(1)} %copy.145) | copy-start | bytes 1572868
  97.0 4.1 %copy-start.8 = (bf16[256,1024]{0,1:T(8,128)(2,1)}, bf16[256,1024]{0,1:T(8,128)(2,1)S(1)}, u32[]{:S(2)}) copy-start(bf16[256,1024]{0,1:T(8,128)(2,1)S(1)} %copy.143) | copy-start | bytes 1572868
  99.3 1.4 copy-start.4
  100.7 3.4 %copy-start.7 = (bf16[256,1024]{0,1:T(8,128)(2,1)S(1)}, bf16[256,1024]{0,1:T(8,128)(2,1)}, u32[]{:S(2)}) copy-start(bf16[256,1024]{0,1:T(8,128)(2,1)} %copy-done.6) | copy-start | bytes 1572868
  101.2 4.2 %copy-start.15 = (f32[1,128,1024]{1,2,0:T(8,128)S(1)}, f32[1,128,1024]{1,2,0:T(8,128)}, u32[]{:S(2)}) copy-start(f32[1,128,1024]{1,2,0:T(8,128)} %copy.147) | copy-start | bytes 1572868
  115.0 4.6 %copy-start.14 = (f32[256,8,64]{0,2,1:T(8,128)S(1)}, f32[256,8,64]{0,2,1:T(8,128)}, u32[]{:S(2)}) copy-start(f32[256,8,64]{0,2,1:T(8,128)} %get-tuple-element.42) | copy-start | bytes 1572868
  115.0 4.7 %copy-start = (bf16[8,256,1024]{2,1,0:T(8,128)(2,1)S(1)}, bf16[8,256,1024]{2,1,0:T(8,128)(2,1)}, u32[]{:S(2)}) copy-start(bf16[8,256,1024]{2,1,0:T(8,128)(2,1)} %exponential_convert_fusion) | copy-start | bytes 12582916
  115.1 4.7 %copy-start.3 = (bf16[1024,1,1,512]{0,3,2,1:T(8,128)(2,1)S(1)}, bf16[1024,1,1,512]{0,3,2,1:T(8,128)(2,1)}, u32[]{:S(2)}) copy-start(bf16[1024,1,1,512]{0,3,2,1:T(8,128)(2,1)} %copy-done.2) | copy-start | bytes 3145732
  119.7 3.9 %copy-start.12 = (bf16[256,1,1,512]{0,3,2,1:T(8,128)(2,1)S(1)}, bf16[256,1,1,512]{0,3,2,1:T(8,128)(2,1)}, u32[]{:S(2)}) copy-start(bf16[256,1,1,512]{0,3,2,1:T(8,128)(2,1)} %copy-done.11) | copy-start | bytes 786436
  121.7 2.0 copy-start.1
  136.4 5.1 %copy-start.10 = (bf16[1,128,1024]{1,2,0:T(8,128)(2,1)S(1)}, bf16[1,128,1024]{1,2,0:T(8,128)(2,1)}, u32[]{:S(2)}) copy-start(bf16[1,128,1024]{1,2,0:T(8,128)(2,1)} %copy-done.9) | copy-start | bytes 786436
  136.4 88.8 %reduce-scatter.5.cloned.1.call-start = ((), (), s32[]{:S(2)}) async-start(), calls=%async_computation.8 | async-start | bytes 2359296 | tf_op jit(solution)/shard_map/reduce_scatter | solution.py:115
  141.8 5.2 %copy-start.19 = (bf16[128,16,64]{0,2,1:T(8,128)(2,1)S(1)}, bf16[128,16,64]{0,2,1:T(8,128)(2,1)}, u32[]{:S(2)}) copy-start(bf16[128,16,64]{0,2,1:T(8,128)(2,1)} %get-tuple-element.47) | copy-start | bytes 786436
  143.2 4.7 %copy-start.16 = (f32[16,64,128]{2,1,0:T(8,128)S(1)}, f32[16,64,128]{2,1,0:T(8,128)}, u32[]{:S(2)}) copy-start(f32[16,64,128]{2,1,0:T(8,128)} %get-tuple-element.46) | copy-start | bytes 1572868
  143.2 4.9 %copy-start.5 = (f32[2,128,1,512]{1,3,0,2:T(8,128)S(1)}, f32[2,128,1,512]{1,3,0,2:T(8,128)}, u32[]{:S(2)}) copy-start(f32[2,128,1,512]{1,3,0,2:T(8,128)} %copy-done.4) | copy-start | bytes 1572868
  183.5 43.3 %all-to-all-start.3 = ((bf16[256,3,1,512]{3,1,2,0:T(4,128)(2,1)}), bf16[256,3,1,512]{3,1,2,0:T(4,128)(2,1)S(1)}, u32[]{:S(2)}, u32[]{:S(2)}) async-start(bf16[256,3,1,512]{3,1,2,0:T(4,128)(2,1)} %copy.154), calls=%async_computation.4 | async-start | bytes 2097152 | tf_op jit(solution)/shard_map/all_to_all | solution.py:171
Sparse Core Ops, SparseCore 0:
  26.0 17.3 all-gather.4
  45.5 16.9 all-gather.6
  136.6 43.8 reduce-scatter.2
  183.9 41.2 reduce-scatter.4
Sparse Core Ops, SparseCore 1:
  30.2 63.0 all-reduce.1
where the time goes:
time: 237 us; the launch traced here: 236 us
  waiting for transfers between devices  110 us (46%)
  local copies, waits for them, and re-layouts  33.4 us (14%)
  matrix products  25.9 us (11%)
  blocking collectives  22.5 us (9%)
  other arithmetic  20 us (8%)
  between operations  16.3 us (7%)
  starting transfers between devices  7.23 us (3%)
    reduce_scatter x1, waiting for transfers between devices, body(): lax.psum_scatter(thermal_sums(cross_probs, cross_dscores, cross_heads, up...  38.1 us
    reduce_scatter x1, waiting for transfers between devices, body(): lax.psum_scatter(jnp.concatenate([key_grad.reshape(lax.axis_size('seq') *...  27.6 us
    psum x1, waiting for transfers between devices, spread(): return lax.psum(block, axis)  18.7 us
    all_to_all x1, blocking collectives, body(): lax.all_to_all(packed, 'head', split_axis=2, concat_axis=0, tiled=True)  14.9 us
    all_gather x1, waiting for transfers between devices, body(): lax.all_gather(by_heads[:, 1, 0], 'seq', axis=0, tiled=True)  13.5 us
    all_gather x1, waiting for transfers between devices, body(): lax.all_gather(by_heads[:, 2, 0], 'seq', axis=0, tiled=True)  11.8 us
    unnamed x50, local copies, waits for them, and re-layouts  7.98 us
    all_to_all x1, blocking collectives, body(): lax.all_to_all(attended_grad.reshape(tokens_here, head_devices, local_wid...  7.56 us
  transfers between devices with their start and end apart: 7, of which 5 were waited for; matrix products, arithmetic and copies ran while one was open for 18% of the time, Pallas kernels for 0%

commit v1 on v0

--- a/solution.py
+++ b/solution.py
@@ -10,7 +10,7 @@
 
 def spread(block, axis, owner):
     block = jnp.where(lax.axis_index(axis) == owner, block, jnp.zeros_like(block))
-    return lax.psum(block, axis)
+    return jnp.sum(lax.all_gather(block, axis), axis=0)
 
 
 def log_total(scores):

time: 237 us -> 266 us (1.12)
  waiting for transfers between devices: 110 us -> 140 us
  other arithmetic: 20 us -> 23.8 us
    all_gather x0 -> x1, waiting for transfers between devices: none -> 33.4 us  [spread(): return jnp.sum(lax.all_gather(block, axis), axis=0)]
    psum x1 -> x0, waiting for transfers between devices: 18.7 us -> none  [spread(): return lax.psum(block, axis)]
    all_to_all x1, waiting for transfers between devices: 0.01 us -> 7.53 us  [body(): lax.all_to_all(attended_heads.reshape(row_count, 1, local_width), 'head',...]
    all_gather x1, waiting for transfers between devices: 11.8 us -> 17.4 us  [body(): lax.all_gather(by_heads[:, 2, 0], 'seq', axis=0, tiled=True)]
    reduce_sum x0 -> x1, other arithmetic: none -> 5.21 us  [spread(): return jnp.sum(lax.all_gather(block, axis), axis=0)]
    unnamed x50 -> x54, local copies, waits for them, and re-layouts: 7.98 us -> 9.2 us
  transfers between devices with their start and end apart: 7 -> 7, of which waited for: 5 -> 6; matrix products, arithmetic and copies ran while one was open for 18% -> 14% of each run, Pallas kernels for 0% -> 0%
where the time goes in v1:
time: 266 us; the launch traced here: 265 us
  waiting for transfers between devices  140 us (53%)
  local copies, waits for them, and re-layouts  32.5 us (12%)
  other arithmetic  23.8 us (9%)
  matrix products  23.3 us (9%)
  blocking collectives  23.1 us (9%)
  between operations  14.9 us (6%)
  starting transfers between devices  7.63 us (3%)
    reduce_scatter x1, waiting for transfers between devices, body(): lax.psum_scatter(thermal_sums(cross_probs, cross_dscores, cross_heads, up...  38.1 us
    all_gather x1, waiting for transfers between devices, spread(): return jnp.sum(lax.all_gather(block, axis), axis=0)  33.4 us
    reduce_scatter x1, waiting for transfers between devices, body(): lax.psum_scatter(jnp.concatenate([key_grad.reshape(lax.axis_size('seq') *...  28.1 us
    all_gather x1, waiting for transfers between devices, body(): lax.all_gather(by_heads[:, 2, 0], 'seq', axis=0, tiled=True)  17.4 us
    all_to_all x1, blocking collectives, body(): lax.all_to_all(packed, 'head', split_axis=2, concat_axis=0, tiled=True)  14.8 us
    all_gather x1, waiting for transfers between devices, body(): lax.all_gather(by_heads[:, 1, 0], 'seq', axis=0, tiled=True)  14.6 us
    unnamed x54, local copies, waits for them, and re-layouts  9.2 us
    all_to_all x1, blocking collectives, body(): lax.all_to_all(attended_grad.reshape(tokens_here, head_devices, local_wid...  8.25 us
  transfers between devices with their start and end apart: 7, of which 6 were waited for; matrix products, arithmetic and copies ran while one was open for 14% of the time, Pallas kernels for 0%

profile of v1, /device:TPU:0, one launch (start us, length us, event | category | flops | bytes accessed | tf_op | source)
XLA Modules:
  0.0 265.1 jit_solution(3998797567958703219)
XLA Ops:
  7.2 1.6 copy.130
  9.1 14.8 %all_to_all.57 = bf16[128,3,2,512]{3,0,1,2:T(8,128)(2,1)S(1)} all-to-all(bf16[128,3,2,512]{3,0,1,2:T(8,128)(2,1)S(1)} %copy.131), channel_id=1, replica_groups=mesh['img'=4,'seq'=4,'head'=2] {'head'}, dimensions={2} | all-to-all | bytes 1572864 | tf_op jit(solution)/shard_map/all_to_all | solution.py:70
  27.6 14.6 %all-gather.7.cloned.1.call-done = bf16[1024,1,1,512]{3,0,1,2:T(8,128)(2,1)} async-done(((bf16[256,1,1,512]{3,0,1,2:T(8,128)(2,1)}), bf16[1024,1,1,512]{3,0,1,2:T(8,128)(2,1)}) %all-gather.7.cloned.1.call-update) | async-done | bytes 1048592 | tf_op jit(solution)/shard_map/all_gather | solution.py:74
  42.2 1.5 copy.134
  43.7 17.4 %all-gather.9.cloned.1.call-done = bf16[1024,1,1,512]{3,0,1,2:T(8,128)(2,1)} async-done(((bf16[256,1,1,512]{3,0,1,2:T(8,128)(2,1)}), bf16[1024,1,1,512]{3,0,1,2:T(8,128)(2,1)}) %all-gather.9.cloned.1.call-update) | async-done | bytes 1048592 | tf_op jit(solution)/shard_map/all_gather | solution.py:75
  61.1 1.5 copy.135
  63.9 1.7 exponential_reduce_fusion
  65.7 1.4 exponential_convert_fusion
  67.1 1.9 copy-done
  69.1 2.2 fusion.10
  73.6 3.4 %all-to-all-start.1 = ((bf16[2,2,32768]{2,1,0:T(2,128)(2,1)}), bf16[2,2,32768]{2,1,0:T(2,128)(2,1)S(1)}, u32[]{:S(2)}, u32[]{:S(2)}) async-start(bf16[2,2,32768]{2,1,0:T(2,128)(2,1)} %reshape.201), calls=%async_computation.1 | async-start | bytes 524288 | tf_op jit(solution)/shard_map/all_to_all | solution.py:91
  78.7 7.5 %all-to-all-done.1 = bf16[2,2,32768]{2,1,0:T(2,128)(2,1)S(1)} async-done(((bf16[2,2,32768]{2,1,0:T(2,128)(2,1)}), bf16[2,2,32768]{2,1,0:T(2,128)(2,1)S(1)}, u32[]{:S(2)}, u32[]{:S(2)}) %all-to-all-start.1) | async-done | bytes 262176 | tf_op jit(solution)/shard_map/all_to_all | solution.py:91
  86.8 33.4 %all-gather.11.cloned.1.call-done = bf16[8,1,256,2048]{3,2,1,0:T(8,128)(2,1)} async-done(((bf16[1,1,256,2048]{3,2,1,0:T(8,128)(2,1)}), bf16[8,1,256,2048]{3,2,1,0:T(8,128)(2,1)}) %all-gather.11.cloned.1.call-update) | async-done | bytes 8388624 | tf_op jit(solution)/shard_map/all_gather | solution.py:13
  120.2 5.2 %reduce_sum.49 = bf16[256,2048]{1,0:T(8,128)(2,1)S(1)} reduce(bf16[8,1,256,2048]{3,2,1,0:T(8,128)(2,1)} %all-gather.11.cloned.1.call-done, bf16[]{:T(256)} %constant.19.clone.1), dimensions={0,1}, to_apply=%region_2.3 | reduce | flops 3670016 | bytes 9437186 | tf_op jit(solution)/shard_map/reduce_sum | solution.py:13
  131.1 1.6 fusion.1
  134.0 8.3 %all_to_all.58 = bf16[128,2,512]{0,2,1:T(8,128)(2,1)S(1)} all-to-all(bf16[128,2,512]{0,2,1:T(8,128)(2,1)S(1)} %add_convert_fusion), channel_id=1, replica_groups=mesh['img'=4,'seq'=4,'head'=2] {'head'}, dimensions={1} | all-to-all | bytes 524288 | tf_op jit(solution)/shard_map/all_to_all | solution.py:129
  144.4 4.5 %fusion.11 = f32[8,64,1024]{2,1,0:T(8,128)} fusion(bf16[256,8,64]{0,2,1:T(8,128)(2,1)S(1)} %reshape_reshape.3, bf16[8,256,1024]{2,1,0:T(8,128)(2,1)} %copy-done), kind=kOutput, calls=%fused_computation.34 | convolution fusion | flops 268435456 | bytes 6553600 | tf_op jit(solution)/shard_map/hqk,qhd->khd/dot_general | solution.py:152
  149.1 1.9 multiply_convert_fusion
  151.0 1.9 copy-done.2
  152.9 2.2 fusion.12
  155.1 2.9 %copy.147 = f32[1024,512]{1,0:T(8,128)} copy(f32[1024,512]{0,1:T(8,128)} %bitcast.103) | data formatting | bytes 4194304 | tf_op jit(solution)/shard_map/reshape | solution.py:158
  158.1 2.9 %copy.148 = f32[1024,512]{1,0:T(8,128)} copy(f32[1024,512]{0,1:T(8,128)} %bitcast.102) | data formatting | bytes 4194304 | tf_op jit(solution)/shard_map/reshape | solution.py:159
  161.0 4.7 %pad_maximum_fusion = f32[1024,1024]{1,0:T(8,128)} fusion(f32[1024,512]{1,0:T(8,128)} %copy.148, f32[1024,512]{1,0:T(8,128)} %copy.147), kind=kLoop, calls=%fused_computation.4 | loop fusion | flops 1048576 | bytes 8388608 | tf_op jit(solution)/shard_map/concatenate | solution.py:156
  166.0 2.5 fusion.4
  168.5 2.6 copy.153
  172.8 3.8 %pad_maximum_fusion.1 = f32[256,2048]{1,0:T(8,128)} fusion(f32[256,1024]{1,0:T(8,128)} %copy.154, f32[256,1024]{1,0:T(8,128)} %copy.153), kind=kLoop, calls=%fused_computation.5 | loop fusion | flops 524288 | bytes 4194304 | tf_op jit(solution)/shard_map/concatenate | solution.py:56
  178.6 3.6 %convolution_convert_fusion = bf16[8,256,64]{1,2,0:T(8,128)(2,1)S(1)} fusion(bf16[8,256,1024]{2,1,0:T(8,128)(2,1)} %copy-done.2, bf16[1024,8,64]{0,2,1:T(8,128)(2,1)S(1)} %bitcast.99), kind=kOutput, calls=%fused_computation.13 | convolution fusion | flops 268566528 | bytes 5505024 | tf_op jit(solution)/shard_map/hqk,khd->qhd/dot_general | solution.py:145
  182.4 28.1 %reduce-scatter.3.cloned.1.call-done = f32[256,1024]{1,0:T(8,128)} async-done(((f32[1024,1024]{1,0:T(8,128)}), f32[256,1024]{1,0:T(8,128)}) %reduce-scatter.3.cloned.1.call-update) | async-done | bytes 1048592 | tf_op jit(solution)/shard_map/reduce_scatter | solution.py:155
  211.9 1.7 copy.150
  213.5 3.6 %all-to-all-start.3 = ((bf16[256,3,1,512]{3,1,2,0:T(4,128)(2,1)}), bf16[256,3,1,512]{3,1,2,0:T(4,128)(2,1)S(1)}, u32[]{:S(2)}, u32[]{:S(2)}) async-start(bf16[256,3,1,512]{3,1,2,0:T(4,128)(2,1)} %copy.150), calls=%async_computation.4 | async-start | bytes 2097152 | tf_op jit(solution)/shard_map/all_to_all | solution.py:171
  217.1 38.1 %reduce-scatter.5.cloned.1.call-done = f32[32,2048]{1,0:T(8,128)} async-done(((f32[256,2048]{1,0:T(8,128)}), f32[32,2048]{1,0:T(8,128)}) %reduce-scatter.5.cloned.1.call-update) | async-done | bytes 262160 | tf_op jit(solution)/shard_map/reduce_scatter | solution.py:115
  255.2 1.6 convert_bitcast_fusion
  (97 shorter events, 25.4 us)
Async XLA Ops:
  7.2 19.2 %copy-start.19 = (bf16[1,1,256,2048]{3,2,1,0:T(8,128)(2,1)S(1)}, bf16[1,1,256,2048]{3,2,1,0:T(8,128)(2,1)}, u32[]{:S(2)}) copy-start(bf16[1,1,256,2048]{3,2,1,0:T(8,128)(2,1)} %param.7) | copy-start | bytes 3145732
  7.2 35.0 %all-gather.7.cloned.1.call-start = ((), (), s32[]{:S(2)}) async-start(), calls=%async_computation.8 | async-start | bytes 1310720 | tf_op jit(solution)/shard_map/all_gather | solution.py:74
  24.9 36.2 %all-gather.9.cloned.1.call-start = ((), (), s32[]{:S(2)}) async-start(), calls=%async_computation.9 | async-start | bytes 1310720 | tf_op jit(solution)/shard_map/all_gather | solution.py:75
  25.6 94.6 %all-gather.11.cloned.1.call-start = ((), (), s32[]{:S(2)}) async-start(), calls=%async_computation.10 | async-start | bytes 9437184 | tf_op jit(solution)/shard_map/all_gather | solution.py:13
  27.6 36.4 %copy-start.12 = (bf16[256,1,1,512]{0,3,2,1:T(8,128)(2,1)}, bf16[256,1,1,512]{0,3,2,1:T(8,128)(2,1)S(1)}, u32[]{:S(2)}) copy-start(bf16[256,1,1,512]{0,3,2,1:T(8,128)(2,1)S(1)} %copy.133) | copy-start | bytes 786436
  62.5 4.6 %copy-start.3 = (bf16[1024,1,1,512]{0,3,2,1:T(8,128)(2,1)}, bf16[1024,1,1,512]{0,3,2,1:T(8,128)(2,1)S(1)}, u32[]{:S(2)}) copy-start(bf16[1024,1,1,512]{0,3,2,1:T(8,128)(2,1)S(1)} %copy.135) | copy-start | bytes 3145732
  67.1 2.0 copy-start
  67.1 10.2 %copy-start.20 = (bf16[1,128,1024]{2,1,0:T(8,128)(2,1)S(1)}, bf16[1,128,1024]{2,1,0:T(8,128)(2,1)}, u32[]{:S(2)}) copy-start(bf16[1,128,1024]{2,1,0:T(8,128)(2,1)} %param.9) | copy-start | bytes 786436
  69.1 9.4 %copy-start.22 = (bf16[1,128,1024]{2,1,0:T(8,128)(2,1)S(1)}, bf16[1,128,1024]{2,1,0:T(8,128)(2,1)}, u32[]{:S(2)}) copy-start(bf16[1,128,1024]{2,1,0:T(8,128)(2,1)} %param.6) | copy-start | bytes 786436
  73.6 12.5 %all-to-all-start.1 = ((bf16[2,2,32768]{2,1,0:T(2,128)(2,1)}), bf16[2,2,32768]{2,1,0:T(2,128)(2,1)S(1)}, u32[]{:S(2)}, u32[]{:S(2)}) async-start(bf16[2,2,32768]{2,1,0:T(2,128)(2,1)} %reshape.201), calls=%async_computation.1 | async-start | bytes 524288 | tf_op jit(solution)/shard_map/all_to_all | solution.py:91
  77.1 133.3 %reduce-scatter.3.cloned.1.call-start = ((), (), s32[]{:S(2)}) async-start(), calls=%async_computation.6 | async-start | bytes 5242880 | tf_op jit(solution)/shard_map/reduce_scatter | solution.py:155
  77.5 53.6 %copy-start.10 = (bf16[1,128,1024]{1,2,0:T(8,128)(2,1)}, bf16[1,128,1024]{1,2,0:T(8,128)(2,1)S(1)}, u32[]{:S(2)}) copy-start(bf16[1,128,1024]{1,2,0:T(8,128)(2,1)S(1)} %copy.144) | copy-start | bytes 786436
  78.6 49.1 %copy-start.14 = (bf16[1,128,1024]{1,2,0:T(8,128)(2,1)}, bf16[1,128,1024]{1,2,0:T(8,128)(2,1)S(1)}, u32[]{:S(2)}) copy-start(bf16[1,128,1024]{1,2,0:T(8,128)(2,1)S(1)} %copy.140) | copy-start | bytes 786436
  86.8 40.9 %copy-start.5 = (f32[2,128,1,512]{1,3,0,2:T(8,128)}, f32[2,128,1,512]{1,3,0,2:T(8,128)S(1)}, u32[]{:S(2)}) copy-start(f32[2,128,1,512]{1,3,0,2:T(8,128)S(1)} %copy.137) | copy-start | bytes 1572868
  127.7 1.4 copy-start.7
  128.3 1.2 copy-start.18
  129.8 1.3 copy-start.9
  129.8 3.0 %copy-start.8 = (bf16[256,1024]{0,1:T(8,128)(2,1)S(1)}, bf16[256,1024]{0,1:T(8,128)(2,1)}, u32[]{:S(2)}) copy-start(bf16[256,1024]{0,1:T(8,128)(2,1)} %copy-done.7) | copy-start | bytes 1572868
  129.8 4.2 %copy-start.16 = (f32[1,128,1024]{1,2,0:T(8,128)S(1)}, f32[1,128,1024]{1,2,0:T(8,128)}, u32[]{:S(2)}) copy-start(f32[1,128,1024]{1,2,0:T(8,128)} %copy.143) | copy-start | bytes 1572868
  144.4 4.6 %copy-start.15 = (f32[256,8,64]{0,2,1:T(8,128)S(1)}, f32[256,8,64]{0,2,1:T(8,128)}, u32[]{:S(2)}) copy-start(f32[256,8,64]{0,2,1:T(8,128)} %get-tuple-element.42) | copy-start | bytes 1572868
  144.4 4.6 %copy-start.1 = (bf16[8,256,1024]{2,1,0:T(8,128)(2,1)S(1)}, bf16[8,256,1024]{2,1,0:T(8,128)(2,1)}, u32[]{:S(2)}) copy-start(bf16[8,256,1024]{2,1,0:T(8,128)(2,1)} %copy-done) | copy-start | bytes 12582916
  144.4 4.6 %copy-start.4 = (bf16[1024,1,1,512]{0,3,2,1:T(8,128)(2,1)S(1)}, bf16[1024,1,1,512]{0,3,2,1:T(8,128)(2,1)}, u32[]{:S(2)}) copy-start(bf16[1024,1,1,512]{0,3,2,1:T(8,128)(2,1)} %copy-done.3) | copy-start | bytes 3145732
  149.0 3.9 %copy-start.13 = (bf16[256,1,1,512]{0,3,2,1:T(8,128)(2,1)S(1)}, bf16[256,1,1,512]{0,3,2,1:T(8,128)(2,1)}, u32[]{:S(2)}) copy-start(bf16[256,1,1,512]{0,3,2,1:T(8,128)(2,1)} %copy-done.12) | copy-start | bytes 786436
  151.0 1.9 copy-start.2
  165.7 5.4 %copy-start.11 = (bf16[1,128,1024]{1,2,0:T(8,128)(2,1)S(1)}, bf16[1,128,1024]{1,2,0:T(8,128)(2,1)}, u32[]{:S(2)}) copy-start(bf16[1,128,1024]{1,2,0:T(8,128)(2,1)} %copy-done.10) | copy-start | bytes 786436
  165.8 89.5 %reduce-scatter.5.cloned.1.call-start = ((), (), s32[]{:S(2)}) async-start(), calls=%async_computation.7 | async-start | bytes 2359296 | tf_op jit(solution)/shard_map/reduce_scatter | solution.py:115
  171.4 5.2 %copy-start.6 = (f32[2,128,1,512]{1,3,0,2:T(8,128)S(1)}, f32[2,128,1,512]{1,3,0,2:T(8,128)}, u32[]{:S(2)}) copy-start(f32[2,128,1,512]{1,3,0,2:T(8,128)} %copy-done.5) | copy-start | bytes 1572868
  172.8 4.0 %copy-start.21 = (bf16[128,16,64]{0,2,1:T(8,128)(2,1)S(1)}, bf16[128,16,64]{0,2,1:T(8,128)(2,1)}, u32[]{:S(2)}) copy-start(bf16[128,16,64]{0,2,1:T(8,128)(2,1)} %get-tuple-element.47) | copy-start | bytes 786436
  172.8 4.9 %copy-start.17 = (f32[16,64,128]{2,1,0:T(8,128)S(1)}, f32[16,64,128]{2,1,0:T(8,128)}, u32[]{:S(2)}) copy-start(f32[16,64,128]{2,1,0:T(8,128)} %get-tuple-element.46) | copy-start | bytes 1572868
  213.5 43.3 %all-to-all-start.3 = ((bf16[256,3,1,512]{3,1,2,0:T(4,128)(2,1)}), bf16[256,3,1,512]{3,1,2,0:T(4,128)(2,1)S(1)}, u32[]{:S(2)}, u32[]{:S(2)}) async-start(bf16[256,3,1,512]{3,1,2,0:T(4,128)(2,1)} %copy.150), calls=%async_computation.4 | async-start | bytes 2097152 | tf_op jit(solution)/shard_map/all_to_all | solution.py:171
Sparse Core Ops, SparseCore 0:
  25.0 17.1 all-gather.6
  44.3 16.7 all-gather.8
  63.0 57.1 all-gather.10
  165.9 44.4 reduce-scatter.2
  213.9 41.2 reduce-scatter.4
